TPU v7x, 32 devices: a whole 2x2x4 slice. The times are simulated.
32 devices in a mesh: ga: 2 (over y), aa: 4 (over x, core), ba: 4 (over z).
Axes of the slice: x: 2, y: 2, z: 4, core: 2. Of those that a mesh axis runs over, the one named last changes fastest.
Arguments:
- query: bfloat16 [2048, 5120], P(('ga', 'aa'), 'ba'), parts along dimension 0, may hold values from -64 to 64
- keys: bfloat16 [16384, 1024], P(('ga', 'aa'), 'ba'), parts along dimension 0, may hold values from -16 to 16
- values: bfloat16 [16384, 1024], P(('ga', 'aa'), 'ba'), parts along dimension 0, may hold values from -6 to 6
- cache_lengths: int32 [8], P(('ga', 'aa')), parts along dimension 0, may hold values from 256 to 2048, as said below
- residual: bfloat16 [2048, 5120], P(('ga', 'ba'), 'aa'), parts along dimension 0, may hold values from -16 to 16
- out_weight: bfloat16 [5120, 5120], P('ba', 'aa'), may hold values from -0.078125 to 0.078125
- norm_gain: float32 [5120], P('aa'), may hold values from 0.1 to 1.9
- router_weight: float32 [5120, 4], P('aa'), may hold values from -0.078125 to 0.078125
- expert_ids: int32 [2048], P(('ga', 'ba')), parts along dimension 0, may hold values from 0 to 3
- expert_slots: int32 [2048], P(('ga', 'ba')), parts along dimension 0, may hold values from -1 to 127, as said below
- expert_gate: bfloat16 [4, 5120, 4096], P('ba', None, 'aa'), may hold values from -0.078125 to 0.078125
- expert_up: bfloat16 [4, 5120, 4096], P('ba', None, 'aa'), may hold values from -0.078125 to 0.078125
- expert_down: bfloat16 [4, 4096, 5120], P('ba', 'aa'), may hold values from -0.25 to 0.25
Outputs:
- layer_out: bfloat16 [2048, 5120], P(('ga', 'ba'), 'aa'), parts along dimension 0
There are 2 independent parts, one for each index of `ga`. A program takes and returns all parts, laid end to end along the dimension named above; an argument that names none is the same for every part. Nothing has to cross between parts.
Inputs may be any that keep to these rules, and one draw needn't show every extreme that they name: `cache_lengths`: some shard has 2048 valid positions in every draw. `expert_slots`: rows form aligned blocks of 256 rows (the rows of one index of ba). A row's slot is the number of earlier rows of its block with the same expert id, or -1 where that number is 128 or more. In every draw some expert has all 128 slots filled in every block.
All inputs are finite; a program needn't handle non-finite values.
Results may differ from a plain program's by a relative error of at most 0.019.
Values may be sent and summed in bfloat16 or wider, within the bound.
A program may use at most 128 MiB of HBM per device.

v0:
```python
import functools

import jax
import jax.numpy as jnp
from jax import lax
from jax.experimental import pallas as pl
from jax.experimental.pallas import tpu as pltpu
from jax.sharding import PartitionSpec as P

D = 5120
HD = 128
Q = 1024
STEP = 1024
LOADS = 4
PARTS = 4
EARLY = 2
PROJECT_GRANT = 67043328
TILE = 256
EXPERTS_GRANT = 67043328
ATTEND_GRANT = 67043328
LANES = 128
LOG2E = 1.4426950408889634


NEGATIVE = -1e30
EPSILON = 1e-05


def attend_kernel(shards, group, *refs):
    lengths, q_ref, refs = refs[:shards], refs[shards], refs[shards + 1 :]
    sources = refs[: 2 * shards]
    out_ref, stat_ref, kv_ref, stack_ref, peak_ref, acc_ref, sems = refs[2 * shards :]
    factor = HD ** (-0.5) * LOG2E
    rows = q_ref.shape[0]
    context = kv_ref.shape[2]
    step = min(STEP, context)
    tails = [size for size in (step // 2, step) if size % LANES == 0]
    g = pl.program_id(0)
    column = pl.ds(pl.multiple_of(g * HD, HD), HD)

    @pl.when(g == 0)
    def _():
        for at, source in enumerate(sources):
            pltpu.make_async_copy(source, kv_ref.at[at // 2, at % 2], sems.at[at // 2, at % 2]).start()

    for head in range(group):
        stack_ref[head * rows : (head + 1) * rows, :] = q_ref[:, head * HD : (head + 1) * HD]
    peak_ref[...] = jnp.full_like(peak_ref, NEGATIVE)
    acc_ref[...] = jnp.zeros_like(acc_ref)

    def chunk(shard, start, size, limit):
        k = kv_ref[shard, 0, pl.ds(start, size), column]
        v = kv_ref[shard, 1, pl.ds(start, size), column]
        v = jnp.concatenate([v, jnp.ones((size, HD), jnp.bfloat16)], axis=1)
        for head in range(group):
            span = slice(head * rows, (head + 1) * rows)
            scores = lax.dot_general(
                stack_ref[span, :], k, (((1,), (1,)), ((), ())), preferred_element_type=jnp.float32
            )
            if limit is not None:
                place = lax.broadcasted_iota(jnp.int32, scores.shape, 1)
                scores = jnp.where(place < limit, scores, NEGATIVE)
            old = peak_ref[span, :]
            new = jnp.maximum(old, jnp.max(scores, axis=1, keepdims=True))
            probs = jnp.exp2((scores - new[:, :1]) * factor).astype(jnp.bfloat16)
            scale = jnp.exp2((old - new) * factor)
            peak_ref[span, :] = new
            acc_ref[span, :] = acc_ref[span, :] * jnp.concatenate([scale, scale], axis=1) + jnp.dot(
                probs, v, preferred_element_type=jnp.float32
            )

    @pl.loop(0, shards)
    def _(shard):
        @pl.when(g == 0)
        def _():
            for part in range(2):
                pltpu.make_async_copy(
                    sources[part], kv_ref.at[shard, part], sems.at[shard, part]
                ).wait()

        length = lengths[0][0]
        for at in range(1, shards):
            length = jnp.where(shard == at, lengths[at][0], length)
        full = length // step
        left = length - full * step
        start = pl.multiple_of(full * step, step)

        @pl.loop(0, full)
        def _(i):
            chunk(shard, pl.multiple_of(i * step, step), step, None)

        low = 0
        for size in tails:

            @pl.when((left > low) & (left <= size))
            def _(size=size):
                chunk(shard, start, size, left)

            low = size

    for head in range(group):
        span = slice(head * rows, (head + 1) * rows)
        out_ref[:, head * HD : (head + 1) * HD] = (acc_ref[span, :HD] / acc_ref[span, HD:]).astype(
            out_ref.dtype
        )
        stat_ref[0, 0, head : head + 1, :] = jnp.transpose(peak_ref[span, :])[0:1, :]
        stat_ref[0, 1, head : head + 1, :] = jnp.transpose(acc_ref[span, HD:])[0:1, :]


def attend(query, key_blocks, value_blocks, lengths, out_type):
    shards = len(key_blocks)
    rows, width = query.shape
    context, kv_width = key_blocks[0].shape
    kv_heads = kv_width // HD
    group = width // HD // kv_heads
    work = shards * rows * width * context
    sources = [array for pair in zip(key_blocks, value_blocks) for array in pair]
    return pl.pallas_call(
        functools.partial(attend_kernel, shards, group),
        grid_spec=pltpu.PrefetchScalarGridSpec(
            num_scalar_prefetch=shards,
            grid=(kv_heads,),
            in_specs=[pl.BlockSpec((rows, group * HD), lambda g, *n: (0, g))]
            + [pl.BlockSpec(memory_space=pl.ANY)] * (2 * shards),
            out_specs=[
                pl.BlockSpec((rows, group * HD), lambda g, *n: (0, g)),
                pl.BlockSpec((1, 2, group, rows), lambda g, *n: (g, 0, 0, 0)),
            ],
            scratch_shapes=[
                pltpu.VMEM((shards, 2, context, kv_width), jnp.bfloat16),
                pltpu.VMEM((group * rows, HD), jnp.bfloat16),
                pltpu.VMEM((group * rows, HD), jnp.float32),
                pltpu.VMEM((group * rows, 2 * HD), jnp.float32),
                pltpu.SemaphoreType.DMA((shards, 2)),
            ],
        ),
        out_shape=[
            jax.ShapeDtypeStruct((rows, width), out_type),
            jax.ShapeDtypeStruct((kv_heads, 2, group, rows), jnp.float32),
        ],
        cost_estimate=pl.CostEstimate(
            flops=4 * work, bytes_accessed=4 * shards * context * kv_heads * HD + 6 * rows * width,
            transcendentals=work // HD,
        ),
        compiler_params=pltpu.CompilerParams(vmem_limit_bytes=ATTEND_GRANT),
        name="attend",
    )(*lengths, query, *sources)


def span_attention(query, keys, values, cache_lengths):
    size = lax.axis_size("aa")
    swap = [(i, i ^ 1) for i in range(size)]
    far = []
    for hop in range(2, size, 2):
        ahead = [(i, (i + hop) % size) for i in range(size)]
        far.append((lax.ppermute(query, "aa", ahead), [(j, i) for i, j in ahead]))
    near_keys = lax.ppermute(keys, "aa", swap)
    near_values = lax.ppermute(values, "aa", swap)
    near_length = lax.ppermute(cache_lengths, "aa", swap)
    parts = [attend(query, [keys], [values], [cache_lengths], jnp.float32)]
    for rows, back in far:
        rows, parts[0] = lax.optimization_barrier((rows, parts[0]))
        out, stat = attend(
            rows,
            [keys, near_keys],
            [values, near_values],
            [cache_lengths, near_length],
            jnp.bfloat16,
        )
        parts.append((lax.ppermute(out, "aa", back), lax.ppermute(stat, "aa", back)))
    parts.append(attend(query, [near_keys], [near_values], [near_length], jnp.float32))
    return merge(parts, keys.shape[1] // HD)


def merge_kernel(count, group, *refs):
    stats, outs, out_ref = refs[:count], refs[count : 2 * count], refs[-1]
    factor = HD ** (-0.5) * LOG2E
    rows = out_ref.shape[0]
    top = functools.reduce(jnp.maximum, [stat[0, 0] for stat in stats])
    weights = [stat[0, 1] * jnp.exp2((stat[0, 0] - top) * factor) for stat in stats]
    whole = functools.reduce(jnp.add, weights)
    shares = [weight / whole for weight in weights]
    for head in range(group):
        span = slice(head * HD, (head + 1) * HD)
        terms = [
            out[:, span].astype(jnp.float32)
            * jnp.transpose(jnp.broadcast_to(share[head : head + 1, :], (HD, rows)))
            for out, share in zip(outs, shares)
        ]
        out_ref[:, span] = functools.reduce(jnp.add, terms).astype(out_ref.dtype)


def merge(parts, kv_heads):
    count = len(parts)
    rows, width = parts[0][0].shape
    group = width // HD // kv_heads
    wide = pl.BlockSpec((rows, group * HD), lambda g: (0, g))
    return pl.pallas_call(
        functools.partial(merge_kernel, count, group),
        grid=(kv_heads,),
        in_specs=[pl.BlockSpec((1, 2, group, rows), lambda g: (g, 0, 0, 0))] * count + [wide] * count,
        out_specs=wide,
        out_shape=jax.ShapeDtypeStruct((rows, width), jnp.bfloat16),
        compiler_params=pltpu.CompilerParams(vmem_limit_bytes=ATTEND_GRANT),
        name="merge",
    )(*[stat for _, stat in parts], *[out for out, _ in parts])


def peers_of(me_a, me_b, n, m):
    peers = [{"ba": lax.rem(me_b + k, m)} for k in range(1, m)]
    peers += [{"aa": lax.rem(me_a + hop, n)} for hop in range(2, n, 2)]
    return peers + [{"aa": partner_of(me_a)}]


def partner_of(me_a):
    return me_a + 1 - 2 * lax.rem(me_a, 2)


def meet(peers):
    barrier = pltpu.get_barrier_semaphore()
    for peer in peers:
        pl.semaphore_signal(barrier, inc=1, device_id=peer, device_id_type=pl.DeviceIdType.MESH)
    pl.semaphore_wait(barrier, len(peers))


def remote(source, target, send, receive, peer):
    copy = pltpu.make_async_remote_copy(
        src_ref=source,
        dst_ref=target,
        send_sem=send,
        recv_sem=receive,
        device_id=peer,
        device_id_type=pl.DeviceIdType.MESH,
    )
    copy.start()
    return copy


def dispatch_kernel(local, n, m, packed, out, own_sem, z_send, z_recv, x_send, x_recv, c_send, c_recv):
    me_a, me_b = lax.axis_index("aa"), lax.axis_index("ba")
    slots, columns = packed.shape[1], packed.shape[2]
    meet(peers_of(me_a, me_b, n, 1 if local else m))

    def index(k):
        return k if local else lax.rem(me_b - k + m, m)

    def place(b, a):
        if len(out.shape) == 3:
            return out.at[a, pl.ds(pl.multiple_of(b * slots, slots), slots)]
        return out.at[
            pl.ds(pl.multiple_of(b * slots, slots), slots),
            pl.ds(pl.multiple_of(a * columns, columns), columns),
        ]

    own = []
    for k in range(m if local else 1):
        own.append(pltpu.make_async_copy(packed.at[index(k)], place(index(k), me_a), own_sem.at[k]))
        own[k].start()
    over_z = [None]
    for k in range(1, 1 if local else m):
        to = lax.rem(me_b + k, m)
        over_z.append(
            remote(packed.at[to], place(me_b, me_a), z_send.at[k], z_recv.at[k], {"ba": to})
        )
    partner = partner_of(me_a)
    over_x, over_c = {}, {}

    def forward(k):
        b = index(k)
        for j, hop in enumerate(range(2, n, 2), 1):
            over_x[k, j].wait_recv()
            block = place(b, lax.rem(me_a - hop + n, n))
            over_c[k, j] = remote(
                block, block, c_send.at[k, j], c_recv.at[k, j], {"aa": partner}
            )

    for k in range(m):
        if k < len(own):
            own[k].wait()
        else:
            over_z[k].wait_recv()
        block = place(index(k), me_a)
        for j, hop in enumerate(range(2, n, 2), 1):
            over_x[k, j] = remote(
                block,
                block,
                x_send.at[k, j],
                x_recv.at[k, j],
                {"aa": lax.rem(me_a + hop, n)},
            )
        over_c[k, 0] = remote(block, block, c_send.at[k, 0], c_recv.at[k, 0], {"aa": partner})
        if k > 0:
            forward(k - 1)
    forward(m - 1)
    for copy in over_c.values():
        copy.wait_recv()
    for copy in over_z[1:] + list(over_x.values()) + list(over_c.values()):
        copy.wait_send()


def dispatch(packed, local, m, name, number):
    n = lax.axis_size("aa")
    columns = packed.shape[1]
    rows = packed.shape[0] // m
    half = n // 2
    sems = [pltpu.SemaphoreType.DMA((m,))] * 2 + [pltpu.SemaphoreType.DMA((m, half))] * 4
    flat = columns % LANES == 0 and not local
    shape = (m * rows, n * columns) if flat else (n, m * rows, columns)
    out = pl.pallas_call(
        functools.partial(dispatch_kernel, local, n, m),
        out_shape=jax.ShapeDtypeStruct(shape, packed.dtype),
        in_specs=[pl.BlockSpec(memory_space=pltpu.VMEM)],
        out_specs=pl.BlockSpec(memory_space=pltpu.VMEM),
        scratch_shapes=[pltpu.SemaphoreType.DMA((m,))] + sems,
        compiler_params=pltpu.CompilerParams(
            collective_id=number, has_side_effects=True, vmem_limit_bytes=24 * 1024 * 1024
        ),
        name=name,
    )(packed.reshape(m, rows, columns))
    if local:
        return out.reshape(n * m * rows, columns)
    return out if flat else out.transpose(1, 0, 2).reshape(m * rows, n * columns)


def combine_kernel(
    n, m, part, out, near, summed, far, total, own_sem, z_send, z_recv, x_send, x_recv, c_send, c_recv
):
    me_a, me_b = lax.axis_index("aa"), lax.axis_index("ba")
    slots, columns = out.shape[1], out.shape[2]
    meet(peers_of(me_a, me_b, n, m))
    partner = partner_of(me_a)

    def piece(k, a):
        b = lax.rem(me_b + k, m)
        if len(part.shape) == 3:
            return part.at[a, pl.ds(pl.multiple_of(b * slots, slots), slots)]
        return part.at[
            pl.ds(pl.multiple_of(b * slots, slots), slots),
            pl.ds(pl.multiple_of(a * columns, columns), columns),
        ]

    order = list(range(1, m)) + [0]
    over_c, over_x = {}, {}
    over_z = [None] * m
    for k in order:
        for j in range(n // 2):
            over_c[k, j] = remote(
                piece(k, lax.rem(partner + 2 * j, n)),
                near.at[k, j],
                c_send.at[k, j],
                c_recv.at[k, j],
                {"aa": partner},
            )

    def join(k, j):
        over_c[k, j].wait_recv()
        mine = piece(k, lax.rem(me_a + 2 * j, n))
        return mine[...].astype(jnp.float32) + near[k, j].astype(jnp.float32)

    def finish(k):
        value = join(k, 0)
        for j in range(1, n // 2):
            over_x[k, j].wait_recv()
            value = value + far[k, j].astype(jnp.float32)
        total[k] = value.astype(total.dtype)
        if k == 0:
            copy = pltpu.make_async_copy(total.at[0], out.at[me_b], own_sem)
            copy.start()
            copy.wait()
        else:
            over_z[k] = remote(
                total.at[k],
                out.at[me_b],
                z_send.at[k],
                z_recv.at[k],
                {"ba": lax.rem(me_b + k, m)},
            )

    for k in order:
        for j in range(1, n // 2):
            summed[k, j] = join(k, j).astype(summed.dtype)
            over_x[k, j] = remote(
                summed.at[k, j],
                far.at[k, j],
                x_send.at[k, j],
                x_recv.at[k, j],
                {"aa": lax.rem(me_a + 2 * j, n)},
            )
    for k in order:
        finish(k)
    for copy in over_z[1:]:
        copy.wait_recv()
    for copy in over_z[1:] + list(over_x.values()) + list(over_c.values()):
        copy.wait_send()


def combine(part):
    n, m = lax.axis_size("aa"), lax.axis_size("ba")
    rows, columns = part.shape[0] // m, part.shape[1] // n
    if columns % LANES:
        part = part.reshape(m * rows, n, columns).transpose(1, 0, 2)
    half = n // 2
    sems = [pltpu.SemaphoreType.DMA((m,))] * 2 + [pltpu.SemaphoreType.DMA((m, half))] * 4
    block = pltpu.VMEM((m, half, rows, columns), part.dtype)
    out = pl.pallas_call(
        functools.partial(combine_kernel, n, m),
        out_shape=jax.ShapeDtypeStruct((m, rows, columns), part.dtype),
        in_specs=[pl.BlockSpec(memory_space=pltpu.VMEM)],
        out_specs=pl.BlockSpec(memory_space=pltpu.VMEM),
        scratch_shapes=[block, block, block, pltpu.VMEM((m, rows, columns), part.dtype)]
        + [pltpu.SemaphoreType.DMA]
        + sems,
        compiler_params=pltpu.CompilerParams(
            collective_id=2, has_side_effects=True, vmem_limit_bytes=40 * 1024 * 1024
        ),
        name="combine",
    )(part)
    return out.reshape(m * rows, columns)


def experts_kernel(
    n,
    m,
    packed,
    gate_hbm,
    up_hbm,
    down_hbm,
    out,
    inputs,
    gate_w,
    up_w,
    down_w,
    sums,
    act,
    part,
    near,
    summed,
    far,
    total,
    load_sem,
    own_sem,
    z_send,
    z_recv,
    x_send,
    x_recv,
    c_send,
    c_recv,
    f_send,
    f_recv,
    bz_send,
    bz_recv,
    bx_send,
    bx_recv,
    bc_send,
    bc_recv,
):
    me_a, me_b = lax.axis_index("aa"), lax.axis_index("ba")
    slots, columns = packed.shape[1], packed.shape[2]
    width = n * columns
    hidden = gate_w.shape[1]
    across, partner = flip(me_a, 2), flip(me_a, 1)
    order = [0, 2, 1, 3]
    block_of = [flip(me_b, way) for way in order]

    loads = []
    for at, (source, target) in enumerate(
        ((gate_hbm, gate_w), (up_hbm, up_w), (down_hbm, down_w))
    ):
        piece = target.shape[0] // LOADS
        for i in range(LOADS):
            rows = pl.ds(i * piece, piece)
            loads.append(
                pltpu.make_async_copy(source.at[0, rows], target.at[rows], load_sem.at[at, i])
            )
            loads[-1].start()
    meet([{"ba": block_of[k]} for k in range(1, m)] + [{"aa": across}, {"aa": partner}])

    def place(k, a):
        return inputs.at[
            k * slots : (k + 1) * slots, pl.ds(pl.multiple_of(a * columns, columns), columns)
        ]

    over_z, over_x, over_c, over_f = {}, {}, {}, {}
    own = pltpu.make_async_copy(packed.at[me_b], place(0, me_a), own_sem)
    for k in range(1, m):
        over_z[k] = remote(
            packed.at[block_of[k]], place(k, me_a), z_send.at[k], z_recv.at[k], {"ba": block_of[k]}
        )

    def spread(k):
        if k:
            over_z[k].wait_recv()
        block = place(k, me_a)
        source = block if k else packed.at[me_b]
        over_x[k] = remote(source, block, x_send.at[k], x_recv.at[k], {"aa": across})
        over_c[k] = remote(source, block, c_send.at[k], c_recv.at[k], {"aa": partner})

    def forward(k):
        over_x[k].wait_recv()
        block = place(k, across)
        over_f[k] = remote(block, block, f_send.at[k], f_recv.at[k], {"aa": partner})

    def dots(pair, half, side, finish):
        rows = slice(2 * pair * slots, 2 * (pair + 1) * slots)
        if side is None:
            deep = slice(0, width)
        else:
            deep = pl.ds(pl.multiple_of(side * (width // 2), width // 2), width // 2)

        @pl.loop(0, hidden // 2 // TILE)
        def _(i):
            span = pl.ds(pl.multiple_of(half * (hidden // 2) + i * TILE, TILE), TILE)
            x = inputs[rows, deep]
            gate = jnp.dot(x, gate_w[deep, span], preferred_element_type=jnp.float32)
            up = jnp.dot(x, up_w[deep, span], preferred_element_type=jnp.float32)
            if not finish:
                sums[0, :, span] = gate
                sums[1, :, span] = up
                return
            if side is not None:
                gate = gate + sums[0, :, span]
                up = up + sums[1, :, span]
            act[rows, span] = (jax.nn.silu(gate) * up).astype(jnp.bfloat16)

    back_c, back_x, back_z = {}, {}, {}

    def lower(pair, a):
        rows = slice(2 * pair * slots, 2 * (pair + 1) * slots)

        @pl.loop(0, columns // TILE)
        def _(i):
            span = pl.ds(pl.multiple_of(a * columns + i * TILE, TILE), TILE)
            part[rows, span] = jnp.dot(
                act[rows, :], down_w[:, span], preferred_element_type=jnp.float32
            ).astype(jnp.bfloat16)

    def piece(k, a):
        return part.at[
            k * slots : (k + 1) * slots, pl.ds(pl.multiple_of(a * columns, columns), columns)
        ]

    def hand(k, j, a):
        back_c[k, j] = remote(
            piece(k, a), near.at[k, j], bc_send.at[k, j], bc_recv.at[k, j], {"aa": partner}
        )

    def join(k, j, a):
        back_c[k, j].wait_recv()
        return piece(k, a)[...].astype(jnp.float32) + near[k, j].astype(jnp.float32)

    def cross(k):
        summed[k] = join(k, 1, across).astype(summed.dtype)
        back_x[k] = remote(
            summed.at[k], far.at[k], bx_send.at[k], bx_recv.at[k], {"aa": across}
        )

    def finish(k):
        value = join(k, 0, me_a)
        back_x[k].wait_recv()
        value = value + far[k].astype(jnp.float32)
        if k == 0:
            out[me_b] = value.astype(out.dtype)
        else:
            total[k] = value.astype(total.dtype)
            back_z[k] = remote(
                total.at[k], out.at[me_b], bz_send.at[k], bz_recv.at[k], {"ba": block_of[k]}
            )

    def descend(pair):
        first, second = 2 * pair + 1, 2 * pair
        lower(pair, flip(partner, 2))
        hand(first, 1, flip(partner, 2))
        hand(second, 1, flip(partner, 2))
        lower(pair, across)
        cross(first)
        cross(second)
        lower(pair, partner)
        hand(first, 0, partner)
        hand(second, 0, partner)
        lower(pair, me_a)

    spread(0)
    own.start()
    forward(0)
    spread(1)
    for copy in loads[: 2 * LOADS]:
        copy.wait()
    own.wait()
    over_c[0].wait_recv()
    over_c[1].wait_recv()
    side = me_a // 2
    dots(0, 0, side, False)
    dots(0, 1, side, False)
    spread(2)
    forward(1)
    over_f[0].wait_recv()
    over_f[1].wait_recv()
    dots(0, 0, 1 - side, True)
    dots(0, 1, 1 - side, True)
    spread(3)
    forward(2)
    for copy in loads[2 * LOADS :]:
        copy.wait()
    descend(0)
    forward(3)
    for k in (2, 3):
        over_c[k].wait_recv()
        over_f[k].wait_recv()
    dots(1, 0, None, True)
    finish(1)
    dots(1, 1, None, True)
    finish(0)
    descend(1)
    finish(3)
    finish(2)
    for copy in back_z.values():
        copy.wait_recv()
    for group in (over_z, over_x, over_c, over_f, back_c, back_x, back_z):
        for copy in group.values():
            copy.wait_send()


def flip(index, way):
    for bit in (1, 2):
        if way & bit:
            index = index + bit - 2 * bit * lax.rem(index // bit, 2)
    return index


def run_experts(packed, gate_w, up_w, down_w):
    n, m = lax.axis_size("aa"), lax.axis_size("ba")
    rows, columns = packed.shape[1:]
    depth, hidden = gate_w.shape[1:]
    block = pltpu.VMEM((m, rows, columns), jnp.bfloat16)
    one, two = pltpu.SemaphoreType.DMA((m,)), pltpu.SemaphoreType.DMA((m, 2))
    out = pl.pallas_call(
        functools.partial(experts_kernel, n, m),
        out_shape=jax.ShapeDtypeStruct((m, rows, columns), jnp.bfloat16),
        in_specs=[pl.BlockSpec(memory_space=pl.ANY)] * 4,
        out_specs=pl.BlockSpec(memory_space=pltpu.VMEM),
        scratch_shapes=[
            pltpu.VMEM((m * rows, n * columns), jnp.bfloat16),
            pltpu.VMEM((depth, hidden), jnp.bfloat16),
            pltpu.VMEM((depth, hidden), jnp.bfloat16),
            pltpu.VMEM((hidden, n * columns), jnp.bfloat16),
            pltpu.VMEM((2, 2 * rows, hidden), jnp.float32),
            pltpu.VMEM((m * rows, hidden), jnp.bfloat16),
            pltpu.VMEM((m * rows, n * columns), jnp.bfloat16),
            pltpu.VMEM((m, 2, rows, columns), jnp.bfloat16),
            block,
            block,
            block,
            pltpu.SemaphoreType.DMA((3, LOADS)),
            pltpu.SemaphoreType.DMA,
        ]
        + [one] * 12
        + [two] * 2,
        compiler_params=pltpu.CompilerParams(
            collective_id=1, has_side_effects=True, vmem_limit_bytes=EXPERTS_GRANT
        ),
        name="experts",
    )(packed, gate_w, up_w, down_w)
    return out.reshape(m * rows, columns)


def plain_experts(packed, gate_w, up_w, down_w):
    piece = dispatch(packed, False, lax.axis_size("ba"), "dispatch", 1)
    gate_part = jnp.dot(piece, gate_w, preferred_element_type=jnp.float32)
    up_part = jnp.dot(piece, up_w, preferred_element_type=jnp.float32)
    act = (jax.nn.silu(gate_part) * up_part).astype(jnp.bfloat16)
    return combine(jnp.dot(act, down_w, preferred_element_type=jnp.float32).astype(jnp.bfloat16))


def project_kernel(
    n,
    m,
    own,
    weight_hbm,
    residual_hbm,
    gain,
    router,
    ids,
    places,
    hidden_hbm,
    packed_hbm,
    gate_hbm,
    hidden,
    packed,
    gate,
    rows_in,
    weight,
    residual,
    up,
    down,
    leaving,
    value,
    stats,
    normed,
    mix,
    placing,
    load_sem,
    store_sem,
    x_send,
    x_recv,
    c_send,
    c_recv,
    f_send,
    f_recv,
    u_send,
    u_recv,
    d_send,
    d_recv,
    s_send,
    s_recv,
):
    me_a, me_b = lax.axis_index("aa"), lax.axis_index("ba")
    rows, columns = hidden.shape
    experts = router.shape[0]
    slots = packed.shape[1]
    part = rows // PARTS
    across, partner = flip(me_a, 2), flip(me_a, 1)
    loads = [
        pltpu.make_async_copy(weight_hbm, weight, load_sem.at[0]),
        pltpu.make_async_copy(residual_hbm, residual, load_sem.at[1]),
        pltpu.make_async_copy(own, rows_in.at[0], load_sem.at[2]),
    ]
    for copy in loads:
        copy.start()
    meet(
        [{"ba": lax.rem(me_b + k, m)} for k in range(1, m)]
        + [{"aa": flip(me_a, way)} for way in range(1, n)]
    )

    def cut(c):
        return pl.ds(pl.multiple_of(c * part, part), part)

    def pass_on(slot, target, sends, receives, peer, c):
        return pltpu.make_async_remote_copy(
            src_ref=(own if target < 3 else rows_in.at[slot]).at[cut(c)],
            dst_ref=rows_in.at[target, cut(c)],
            send_sem=sends.at[c],
            recv_sem=receives.at[c],
            device_id={"aa": peer},
            device_id_type=pl.DeviceIdType.MESH,
        )

    over_x = functools.partial(pass_on, 0, 2, x_send, x_recv, across)
    over_c = functools.partial(pass_on, 0, 1, c_send, c_recv, partner)
    over_f = functools.partial(pass_on, 2, 3, f_send, f_recv, partner)
    for c in range(PARTS):
        over_x(c).start()
    for c in range(PARTS):
        over_c(c).start()
    half, low = me_b // 2, lax.rem(me_b, 2)
    order = [3 - 3 * half, 2 - half, 2 * half + 1 - low, me_b]

    def climb(b, c, target):
        return pltpu.make_async_remote_copy(
            src_ref=leaving.at[b, cut(c)],
            dst_ref=up.at[b, cut(c)],
            send_sem=u_send.at[b, c],
            recv_sem=u_recv.at[b, c],
            device_id={"ba": target},
            device_id_type=pl.DeviceIdType.MESH,
        )

    def sink(b, c, target):
        return pltpu.make_async_remote_copy(
            src_ref=leaving.at[b, cut(c)],
            dst_ref=down.at[b, cut(c)],
            send_sem=d_send.at[b, c],
            recv_sem=d_recv.at[b, c],
            device_id={"ba": target},
            device_id_type=pl.DeviceIdType.MESH,
        )

    above, below = lax.rem(me_b + 1, m), lax.rem(me_b + m - 1, m)
    for copy in (loads[2], loads[0]):
        copy.wait()

    def step(at, c):
        b = order[at]
        slot = lax.rem(b // 2 + me_a // 2, 2) * 2 + lax.rem(b + me_a, 2)
        value[...] = jnp.dot(
            rows_in[slot, cut(c), :], weight[...], preferred_element_type=jnp.float32
        )

        @pl.when((b >= me_b) & (me_b > 0))
        def _():
            climb(b, c, above).wait_recv()
            value[...] += up[b, cut(c), :].astype(jnp.float32)

        @pl.when((b <= me_b) & (me_b < m - 1))
        def _():
            sink(b, c, below).wait_recv()
            value[...] += down[b, cut(c), :].astype(jnp.float32)

        if at == m - 1:
            hidden[cut(c), :] = residual[cut(c), :].astype(jnp.float32) + value[...]
            return
        leaving[b, cut(c), :] = value[...].astype(leaving.dtype)

        @pl.when(b > me_b)
        def _():
            climb(b, c, above).start()

        @pl.when(b < me_b)
        def _():
            sink(b, c, below).start()

    place = jnp.where(places[...] >= 0, ids[...] * slots + places[...], -1)
    placing[...] = (
        lax.broadcasted_iota(jnp.int32, placing.shape, 0) == place
    ).astype(jnp.bfloat16)
    for c in range(PARTS):
        over_c(c).wait_recv()
    edge = (me_b == 0) | (me_b == m - 1)
    early = edge & (order[0] // 2 != me_a // 2)

    @pl.when(early)
    def _():
        @pl.loop(0, EARLY)
        def _(c):
            step(2, c)

    @pl.loop(0, PARTS)
    def _(c):
        over_x(c).wait_recv()
        over_f(c).start()
        over_f(c).wait_recv()
        step(0, c)

    @pl.loop(0, PARTS)
    def _(c):
        step(1, c)

        @pl.when((early & (c < EARLY)) == False)
        def _():
            step(2, c)

    loads[1].wait()

    @pl.loop(0, PARTS)
    def _(c):
        step(3, c)
        kept = hidden[cut(c), :]
        lane = lax.broadcasted_iota(jnp.int32, (part, LANES), 1)
        square = jnp.sum(kept * kept, axis=1, keepdims=True)
        found = jnp.where(lane == experts, square, 0.0)
        scaled = kept * gain[...]
        for e in range(experts):
            logit = jnp.sum(scaled * router[e : e + 1, :], axis=1, keepdims=True)
            found = jnp.where(lane == e, logit, found)
        mix[cut(c), :] = found

    stores = [pltpu.make_async_copy(hidden, hidden_hbm, store_sem.at[m])]
    stores[0].start()
    stats[0] = jnp.transpose(mix[...])[: stats.shape[1], :]
    over_s = [
        remote(
            stats.at[0],
            stats.at[way],
            s_send.at[way],
            s_recv.at[way],
            {"aa": flip(me_a, way)},
        )
        for way in range(1, n)
    ]
    for copy in over_s:
        copy.wait_recv()
    sums = functools.reduce(jnp.add, [stats[way] for way in range(n)])
    inverse = 1.0 / jnp.sqrt(sums[experts : experts + 1, :] / (n * columns) + EPSILON)
    chosen = ids[...] == lax.broadcasted_iota(jnp.int32, (experts, rows), 0)
    gate[...] = jnp.sum(
        jnp.where(chosen, jax.nn.sigmoid(sums[:experts, :] * inverse), 0.0), axis=0, keepdims=True
    )
    stores.append(pltpu.make_async_copy(gate, gate_hbm, store_sem.at[m + 1]))
    stores[-1].start()
    spread = jnp.transpose(jnp.broadcast_to(inverse, (LANES, rows)))
    for at in range(0, columns, LANES):
        span = slice(at, at + LANES)
        normed[:, span] = (hidden[:, span] * spread * gain[:, span]).astype(jnp.bfloat16)
    for b in range(m):
        packed[b] = jnp.dot(
            placing[b * slots : (b + 1) * slots, :],
            normed[...],
            preferred_element_type=jnp.float32,
        ).astype(packed.dtype)
        stores.append(pltpu.make_async_copy(packed.at[b], packed_hbm.at[b], store_sem.at[b]))
        stores[-1].start()
    for copy in over_s:
        copy.wait_send()

    @pl.loop(0, PARTS)
    def _(c):
        for copy in (over_x, over_c, over_f):
            copy(c).wait_send()
        for at in range(m - 1):

            @pl.when(order[at] > me_b)
            def _(b=order[at], c=c):
                climb(b, c, above).wait_send()

            @pl.when(order[at] < me_b)
            def _(b=order[at], c=c):
                sink(b, c, below).wait_send()

    for copy in stores:
        copy.wait()


def project(own, weight, residual, gain, router, ids, places):
    n, m = lax.axis_size("aa"), lax.axis_size("ba")
    rows, columns = residual.shape
    experts = router.shape[1]
    slots = 2 * rows // experts
    block = pltpu.VMEM((m, rows, columns), jnp.bfloat16)
    one, two = pltpu.SemaphoreType.DMA((PARTS,)), pltpu.SemaphoreType.DMA((m, PARTS))
    vmem, anywhere = pl.BlockSpec(memory_space=pltpu.VMEM), pl.BlockSpec(memory_space=pl.ANY)
    return pl.pallas_call(
        functools.partial(project_kernel, n, m),
        out_shape=[
            jax.ShapeDtypeStruct((rows, columns), jnp.float32),
            jax.ShapeDtypeStruct((m, slots, columns), jnp.bfloat16),
            jax.ShapeDtypeStruct((1, rows), jnp.float32),
        ],
        in_specs=[anywhere, anywhere, anywhere, vmem, vmem, vmem, vmem],
        out_specs=[anywhere] * 3,
        scratch_shapes=[
            pltpu.VMEM((rows, columns), jnp.float32),
            pltpu.VMEM((m, slots, columns), jnp.bfloat16),
            pltpu.VMEM((1, rows), jnp.float32),
            pltpu.VMEM((n, rows, own.shape[1]), jnp.bfloat16),
            pltpu.VMEM(weight.shape, jnp.bfloat16),
            pltpu.VMEM((rows, columns), jnp.bfloat16),
            block,
            block,
            block,
            pltpu.VMEM((rows // PARTS, columns), jnp.float32),
            pltpu.VMEM((n, 8, rows), jnp.float32),
            pltpu.VMEM((rows, columns), jnp.bfloat16),
            pltpu.VMEM((rows, LANES), jnp.float32),
            pltpu.VMEM((m * slots, rows), jnp.bfloat16),
            pltpu.SemaphoreType.DMA((3,)),
            pltpu.SemaphoreType.DMA((m + 2,)),
        ]
        + [one] * 6
        + [two] * 4
        + [pltpu.SemaphoreType.DMA((n,))] * 2,
        compiler_params=pltpu.CompilerParams(
            collective_id=4, has_side_effects=True, vmem_limit_bytes=PROJECT_GRANT
        ),
        name="project",
    )(
        own,
        weight,
        residual,
        gain.reshape(1, columns),
        router.T,
        ids.reshape(1, rows),
        places.reshape(1, rows),
    )


def placing_of(expert_ids, expert_slots, experts):
    slot_count = 2 * expert_ids.shape[0] // experts
    combined = expert_ids * slot_count + expert_slots
    placing = (
        combined[:, None] == lax.broadcasted_iota(jnp.int32, (1, experts * slot_count), 1)
    ) & (expert_slots[:, None] >= 0)
    return placing.astype(jnp.bfloat16)


def plain_project(
    own, out_weight, residual, norm_gain, router_weight, expert_ids, expert_slots
):
    attended = dispatch(own, True, 4 if own.shape[0] % 64 == 0 else 1, "gather", 3)
    hidden = residual.astype(jnp.float32) + lax.psum_scatter(
        jnp.dot(attended, out_weight, preferred_element_type=jnp.float32).astype(jnp.bfloat16),
        "ba",
        scatter_dimension=0,
        tiled=True,
    ).astype(jnp.float32)
    scaled = hidden * norm_gain
    sums = lax.psum(
        jnp.concatenate(
            [
                jnp.dot(scaled, router_weight, precision=lax.Precision.HIGHEST),
                jnp.sum(hidden * hidden, axis=1, keepdims=True),
            ],
            axis=1,
        ),
        "aa",
    )
    inverse = 1.0 / jnp.sqrt(sums[:, -1] / D + EPSILON)
    normed = scaled * inverse[:, None]
    logits = sums[:, :-1] * inverse[:, None]
    experts = router_weight.shape[1]
    chosen = expert_ids[:, None] == lax.broadcasted_iota(jnp.int32, (1, experts), 1)
    gate = jnp.sum(jnp.where(chosen, jax.nn.sigmoid(logits), 0.0), axis=1)
    expert_in = normed.astype(jnp.bfloat16)
    placing = placing_of(expert_ids, expert_slots, experts)
    packed = lax.dot_general(
        placing, expert_in, (((0,), (0,)), ((), ())), preferred_element_type=jnp.float32
    ).astype(jnp.bfloat16)
    return hidden, packed, gate


def on_device(
    query,
    keys,
    values,
    cache_lengths,
    residual,
    out_weight,
    norm_gain,
    router_weight,
    expert_ids,
    expert_slots,
    expert_gate,
    expert_up,
    expert_down,
):
    own = span_attention(query, keys, values, cache_lengths)
    n, m = lax.axis_size("aa"), lax.axis_size("ba")
    experts = router_weight.shape[1]
    rows, columns = residual.shape
    if n == 4 and m == 4 and experts == m and own.shape[0] == rows and columns % LANES == 0:
        hidden, packed, gate = project(
            own, out_weight, residual, norm_gain, router_weight, expert_ids, expert_slots
        )
        returned = run_experts(packed, expert_gate, expert_up, expert_down)
        gate = gate[0]
    else:
        hidden, packed, gate = plain_project(
            own, out_weight, residual, norm_gain, router_weight, expert_ids, expert_slots
        )
        returned = plain_experts(packed, expert_gate[0], expert_up[0], expert_down[0])
    placing = placing_of(expert_ids, expert_slots, experts)
    from_experts = jnp.dot(placing, returned, preferred_element_type=jnp.float32)
    return (hidden + gate[:, None] * from_experts).astype(jnp.bfloat16)


def solution(mesh):
    return jax.shard_map(
        on_device,
        mesh=mesh,
        in_specs=(
            P(("ga", "aa"), "ba"),
            P(("ga", "aa"), "ba"),
            P(("ga", "aa"), "ba"),
            P(("ga", "aa")),
            P(("ga", "ba"), "aa"),
            P("ba", "aa"),
            P("aa"),
            P("aa", None),
            P(("ga", "ba")),
            P(("ga", "ba")),
            P("ba", None, "aa"),
            P("ba", None, "aa"),
            P("ba", "aa", None),
        ),
        out_specs=P(("ga", "ba"), "aa"),
        check_vma=False,
    )
```

profile of v0, /device:TPU:0, one launch (start us, length us, event | category | flops | bytes accessed | tf_op | source)
XLA Modules:
  0.0 214.6 jit_solution(16593505854296366232)
XLA Ops:
  0.0 0.5 collective-permute-start.2
  0.5 0.0 collective-permute-start.3
  0.5 3.0 %collective-permute-start = (bf16[256,1280]{1,0:T(8,128)(2,1)}, bf16[256,1280]{1,0:T(8,128)(2,1)}, u32[]{:S(2)}, u32[]{:S(2)}) collective-permute-start(bf16[256,1280]{1,0:T(8,128)(2,1)} %refs_1_.3), channel_id=1, source_target_pairs={{0,8},{4,12},{8,0},{12,4},{1,9},{5,13},{9,1},{13,5},{2,10},{6,14},... | collective-permute-start | bytes 1966088 | tf_op jit(solution)/shard_map/ppermute | solution.py:156
  3.5 0.0 collective-permute-start.1
  4.1 1.3 reshape.16.gain
  5.4 9.0 %attend.3 = (f32[256,1280]{1,0:T(8,128)}, f32[2,2,5,256]{3,2,1,0:T(8,128)}) custom-call(s32[1]{0:T(128)S(6)} %copy.14.refs_0_, bf16[256,1280]{1,0:T(8,128)(2,1)} %refs_1_.3, bf16[2048,256]{1,0:T(8,128)(2,1)} %refs_3_.3, bf16[2048,256]{1,0:T(8,128)(2,1)} %refs_4_.1), custom_call_target="tpu_custom_call" | custom-call | flops 2684354560 | bytes 4063232 | tf_op jit(solution)/shard_map/attend/pallas_call | solution.py:118
  14.5 4.2 %collective-permute-done.refs_2_ = bf16[256,1280]{1,0:T(8,128)(2,1)} collective-permute-done((bf16[256,1280]{1,0:T(8,128)(2,1)}, bf16[256,1280]{1,0:T(8,128)(2,1)}, u32[]{:S(2)}, u32[]{:S(2)}) %collective-permute-start) | collective-permute-done | bytes 655392 | tf_op jit(solution)/shard_map/ppermute | solution.py:156
  18.7 0.0 collective-permute-done.1.refs_1_.refs_0_
  18.7 0.0 collective-permute-done.2.refs_5_.refs_2_
  18.7 0.0 collective-permute-done.3.refs_6_.refs_3_
  18.7 14.3 %attend.4 = (bf16[256,1280]{1,0:T(8,128)(2,1)}, f32[2,2,5,256]{3,2,1,0:T(8,128)}) custom-call(s32[1]{0:T(128)S(6)} %copy.14.refs_0_, s32[1]{0:T(128)} %collective-permute-done.1.refs_1_.refs_0_, bf16[256,1280]{1,0:T(8,128)(2,1)} %collective-permute-done.refs_2_, bf16[2048,256]{1,0:T(8,128)(2,1)} %refs_3_.3, bf16[2048,256]{1,0:T(8,128)(2,1)} %refs_4_.1, ...), custom_call_target="tpu_custom_call" | custom-call | flops 5368709120 | bytes 6160384 | tf_op jit(solution)/shard_map/attend/pallas_call | solution.py:118
  33.1 10.4 %collective-permute-start.5 = (bf16[256,1280]{1,0:T(8,128)(2,1)}, bf16[256,1280]{1,0:T(8,128)(2,1)}, u32[]{:S(2)}, u32[]{:S(2)}) collective-permute-start(bf16[256,1280]{1,0:T(8,128)(2,1)} %get-tuple-element.24), channel_id=1, source_target_pairs={{8,0},{12,4},{0,8},{4,12},{9,1},{13,5},{1,9},{5,13},{10,2},{14,6},... | collective-permute-start | bytes 1966088 | tf_op jit(solution)/shard_map/ppermute | solution.py:170
  43.5 1.2 broadcast_compare_fusion
  44.7 1.3 multiply_add_fusion
  45.9 0.0 collective-permute-start.4
  45.9 9.9 %attend.5 = (f32[256,1280]{1,0:T(8,128)}, f32[2,2,5,256]{3,2,1,0:T(8,128)}) custom-call(s32[1]{0:T(128)} %collective-permute-done.1.refs_1_.refs_0_, bf16[256,1280]{1,0:T(8,128)(2,1)} %refs_1_.3, bf16[2048,256]{1,0:T(8,128)(2,1)} %collective-permute-done.2.refs_5_.refs_2_, bf16[2048,256]{1,0:T(8,128)(2,1)} %collective-permute-done.3.refs_6_.refs_3_), custom_call_target="tpu_custom_call" | custom-call | flops 2684354560 | bytes 4063232 | tf_op jit(solution)/shard_map/attend/pallas_call | solution.py:118
  55.8 2.7 %collective-permute-done.4.refs_1_ = f32[2,2,5,256]{3,2,1,0:T(8,128)} collective-permute-done((f32[2,2,5,256]{3,2,1,0:T(8,128)}, f32[2,2,5,256]{3,2,1,0:T(8,128)}, u32[]{:S(2)}, u32[]{:S(2)}) %collective-permute-start.4) | collective-permute-done | bytes 20512 | tf_op jit(solution)/shard_map/ppermute | solution.py:170
  58.5 0.0 collective-permute-done.5.refs_4_
  58.5 3.4 %merge.1.own = bf16[256,1280]{1,0:T(8,128)(2,1)} custom-call(f32[2,2,5,256]{3,2,1,0:T(8,128)} %get-tuple-element.19.refs_0_, f32[2,2,5,256]{3,2,1,0:T(8,128)} %collective-permute-done.4.refs_1_, f32[2,2,5,256]{3,2,1,0:T(8,128)} %get-tuple-element.22.refs_2_, f32[256,1280]{1,0:T(8,128)} %get-tuple-element.23.refs_3_, ...), custom_call_target="tpu_custom_call" | custom-call | tf_op jit(solution)/shard_map/merge/pallas_call | solution.py:198
  61.9 64.0 %project.1 = (f32[256,1280]{1,0:T(8,128)}, bf16[4,128,1280]{2,1,0:T(8,128)(2,1)}, f32[1,256]{1,0:T(1,128)}) custom-call(bf16[256,1280]{1,0:T(8,128)(2,1)} %merge.1.own, bf16[1280,1280]{1,0:T(8,128)(2,1)} %weight_hbm.1, bf16[256,1280]{1,0:T(8,128)(2,1)} %residual_hbm.1, f32[1,1280]{1,0:T(1,128)} %reshape.16.gain, f32[4,1280]{1,0:T(4,128)} %bitcast.7, ...), custom_call_target="tpu_custom_call" | custom-call | tf_op jit(solution)/shard_map/project/pallas_call | solution.py:920
  126.0 85.6 %experts.1 = bf16[4,128,1280]{2,1,0:T(8,128)(2,1)} custom-call(bf16[4,128,1280]{2,1,0:T(8,128)(2,1)} %get-tuple-element.28.packed, bf16[1,5120,1024]{2,1,0:T(8,128)(2,1)} %gate_hbm.1, bf16[1,5120,1024]{2,1,0:T(8,128)(2,1)} %up_hbm.1, bf16[1,1024,5120]{2,1,0:T(8,128)(2,1)} %down_hbm.1), custom_call_target="tpu_custom_call" | custom-call | tf_op jit(solution)/shard_map/experts/pallas_call | solution.py:636
  211.6 0.0 copy-start
  211.6 0.0 copy-start.1
  211.6 2.0 fusion.1
  213.6 0.0 copy-done
  213.6 0.0 copy-done.1
  213.6 1.0 add_convert_fusion
Async XLA Ops:
  0.0 18.7 %collective-permute-start.2 = (bf16[2048,256]{1,0:T(8,128)(2,1)}, bf16[2048,256]{1,0:T(8,128)(2,1)}, u32[]{:S(2)}, u32[]{:S(2)}) collective-permute-start(bf16[2048,256]{1,0:T(8,128)(2,1)} %refs_3_.3), channel_id=1, source_target_pairs={{0,4},{4,0},{8,12},{12,8},{1,5},{5,1},{9,13},{13,9},{2,6},{6,2},{1... | collective-permute-start | bytes 3145736 | tf_op jit(solution)/shard_map/ppermute | solution.py:157
  0.5 18.2 %collective-permute-start.3 = (bf16[2048,256]{1,0:T(8,128)(2,1)}, bf16[2048,256]{1,0:T(8,128)(2,1)}, u32[]{:S(2)}, u32[]{:S(2)}) collective-permute-start(bf16[2048,256]{1,0:T(8,128)(2,1)} %refs_4_.1), channel_id=1, source_target_pairs={{0,4},{4,0},{8,12},{12,8},{1,5},{5,1},{9,13},{13,9},{2,6},{6,2},{1... | collective-permute-start | bytes 3145736 | tf_op jit(solution)/shard_map/ppermute | solution.py:158
  0.5 18.2 %collective-permute-start = (bf16[256,1280]{1,0:T(8,128)(2,1)}, bf16[256,1280]{1,0:T(8,128)(2,1)}, u32[]{:S(2)}, u32[]{:S(2)}) collective-permute-start(bf16[256,1280]{1,0:T(8,128)(2,1)} %refs_1_.3), channel_id=1, source_target_pairs={{0,8},{4,12},{8,0},{12,4},{1,9},{5,13},{9,1},{13,5},{2,10},{6,14},... | collective-permute-start | bytes 1966088 | tf_op jit(solution)/shard_map/ppermute | solution.py:156
  3.5 15.2 %collective-permute-start.1 = (s32[1]{0:T(128)}, s32[1]{0:T(128)}, u32[]{:S(2)}, u32[]{:S(2)}) collective-permute-start(s32[1]{0:T(128)} %param.16), channel_id=1, source_target_pairs={{0,4},{4,0},{8,12},{12,8},{1,5},{5,1},{9,13},{13,9},{2,6},{6,2},{1... | collective-permute-start | bytes 20 | tf_op jit(solution)/shard_map/ppermute | solution.py:159
  33.1 25.5 %collective-permute-start.5 = (bf16[256,1280]{1,0:T(8,128)(2,1)}, bf16[256,1280]{1,0:T(8,128)(2,1)}, u32[]{:S(2)}, u32[]{:S(2)}) collective-permute-start(bf16[256,1280]{1,0:T(8,128)(2,1)} %get-tuple-element.24), channel_id=1, source_target_pairs={{8,0},{12,4},{0,8},{4,12},{9,1},{13,5},{1,9},{5,13},{10,2},{14,6},... | collective-permute-start | bytes 1966088 | tf_op jit(solution)/shard_map/ppermute | solution.py:170
  45.9 12.6 %collective-permute-start.4 = (f32[2,2,5,256]{3,2,1,0:T(8,128)}, f32[2,2,5,256]{3,2,1,0:T(8,128)}, u32[]{:S(2)}, u32[]{:S(2)}) collective-permute-start(f32[2,2,5,256]{3,2,1,0:T(8,128)} %get-tuple-element.21), channel_id=1, source_target_pairs={{8,0},{12,4},{0,8},{4,12},{9,1},{13,5},{1,9},{5,13},{10,2},{14,6},... | collective-permute-start | bytes 61448 | tf_op jit(solution)/shard_map/ppermute | solution.py:170
  211.6 2.0 copy-start
  211.6 2.0 copy-start.1
where the time goes:
time: 215 us
  Pallas kernels  186 us (87%)
  starting transfers between devices  13.9 us (6%)
  waiting for transfers between devices  6.93 us (3%)
  other arithmetic  3.5 us (2%)
    pallas_call x1, Pallas kernels, run_experts(): pl.pallas_call(functools.partial(experts_kernel, n, m), out_shape=jax.Sha...  85.6 us
    pallas_call x1, Pallas kernels, project(): pl.pallas_call(functools.partial(project_kernel, n, m), out_shape=[jax.Sh...  64 us
    pallas_call x3, Pallas kernels, attend(): pl.pallas_call(functools.partial(attend_kernel, shards, group), grid_spec...  33.2 us
    ppermute x1, starting transfers between devices, span_attention(): lax.ppermute(out, 'aa', back)  10.4 us
  transfers between devices with their start and end apart: 6, of which 2 were waited for; matrix products, arithmetic and copies ran while one was open for 2% of the time, Pallas kernels for 9%

commit v1 on v0

--- a/solution.py
+++ b/solution.py
@@ -34,7 +34,7 @@
     rows = q_ref.shape[0]
     context = kv_ref.shape[2]
     step = min(STEP, context)
-    tails = [size for size in (step // 2, step) if size % LANES == 0]
+    tails = [size for size in (step // 4, step // 2, step) if size % LANES == 0]
     g = pl.program_id(0)
     column = pl.ds(pl.multiple_of(g * HD, HD), HD)
 
@@ -544,27 +544,44 @@
             piece(k, a), near.at[k, j], bc_send.at[k, j], bc_recv.at[k, j], {"aa": partner}
         )
 
-    def join(k, j, a):
-        back_c[k, j].wait_recv()
-        return piece(k, a)[...].astype(jnp.float32) + near[k, j].astype(jnp.float32)
+    def join(k, j, a, h):
+        rows = slice(h * slots // 2, (h + 1) * slots // 2)
+        mine = part[
+            k * slots + rows.start : k * slots + rows.stop,
+            pl.ds(pl.multiple_of(a * columns, columns), columns),
+        ]
+        return rows, mine.astype(jnp.float32) + near[k, j, rows].astype(jnp.float32)
 
     def cross(k):
-        summed[k] = join(k, 1, across).astype(summed.dtype)
-        back_x[k] = remote(
-            summed.at[k], far.at[k], bx_send.at[k], bx_recv.at[k], {"aa": across}
-        )
+        back_c[k, 1].wait_recv()
+        for h in range(2):
+            rows, value = join(k, 1, across, h)
+            summed[k, rows] = value.astype(summed.dtype)
+            back_x[k, h] = remote(
+                summed.at[k, rows],
+                far.at[k, rows],
+                bx_send.at[k, h],
+                bx_recv.at[k, h],
+                {"aa": across},
+            )
 
     def finish(k):
-        value = join(k, 0, me_a)
-        back_x[k].wait_recv()
-        value = value + far[k].astype(jnp.float32)
-        if k == 0:
-            out[me_b] = value.astype(out.dtype)
-        else:
-            total[k] = value.astype(total.dtype)
-            back_z[k] = remote(
-                total.at[k], out.at[me_b], bz_send.at[k], bz_recv.at[k], {"ba": block_of[k]}
-            )
+        back_c[k, 0].wait_recv()
+        for h in range(2):
+            rows, value = join(k, 0, me_a, h)
+            back_x[k, h].wait_recv()
+            value = value + far[k, rows].astype(jnp.float32)
+            if k == 0:
+                out[me_b, rows] = value.astype(out.dtype)
+            else:
+                total[k, rows] = value.astype(total.dtype)
+                back_z[k, h] = remote(
+                    total.at[k, rows],
+                    out.at[me_b, rows],
+                    bz_send.at[k, h],
+                    bz_recv.at[k, h],
+                    {"ba": block_of[k]},
+                )
 
     def descend(pair):
         first, second = 2 * pair + 1, 2 * pair
@@ -653,8 +670,8 @@
             pltpu.SemaphoreType.DMA((3, LOADS)),
             pltpu.SemaphoreType.DMA,
         ]
-        + [one] * 12
-        + [two] * 2,
+        + [one] * 8
+        + [two] * 6,
         compiler_params=pltpu.CompilerParams(
             collective_id=1, has_side_effects=True, vmem_limit_bytes=EXPERTS_GRANT
         ),

time: 215 us -> 213 us (level); the launches traced: 215 us -> 210 us
  Pallas kernels: 186 us -> 197 us
  starting transfers between devices: 13.9 us -> 5.56 us
  waiting for transfers between devices: 6.93 us -> 0.02 us
    pallas_call x3, Pallas kernels: 33.2 us -> 47.7 us  [attend(): pl.pallas_call(functools.partial(attend_kernel, shards, group), grid_spec...]
    ppermute x1, starting transfers between devices: 10.4 us -> 0.07 us  [span_attention(): lax.ppermute(out, 'aa', back)]
    ppermute x1, waiting for transfers between devices: 4.21 us -> 0.01 us  [span_attention(): far.append((lax.ppermute(query, 'aa', ahead), [(j, i) for i, j in ahead]))]
    pallas_call x1, Pallas kernels: 85.6 us -> 81.7 us  [run_experts(): pl.pallas_call(functools.partial(experts_kernel, n, m), out_shape=jax.Sha...]
    ppermute x1, waiting for transfers between devices: 2.71 us -> 0.01 us  [span_attention(): lax.ppermute(stat, 'aa', back)]
  transfers between devices with their start and end apart: 6 -> 6, of which waited for: 2 -> 0; matrix products, arithmetic and copies ran while one was open for 2% -> 2% of each run, Pallas kernels for 9% -> 12%
where the time goes in v1:
time: 213 us; the launch traced here: 210 us
  Pallas kernels  197 us (92%)
  starting transfers between devices  5.56 us (3%)
  other arithmetic  3.5 us (2%)
    pallas_call x1, Pallas kernels, run_experts(): pl.pallas_call(functools.partial(experts_kernel, n, m), out_shape=jax.Sha...  81.7 us
    pallas_call x1, Pallas kernels, project(): pl.pallas_call(functools.partial(project_kernel, n, m), out_shape=[jax.Sh...  64.1 us
    pallas_call x3, Pallas kernels, attend(): pl.pallas_call(functools.partial(attend_kernel, shards, group), grid_spec...  47.7 us
  transfers between devices with their start and end apart: 6, of which 0 were waited for; matrix products, arithmetic and copies ran while one was open for 2% of the time, Pallas kernels for 12%

profile of v1, /device:TPU:0, one launch (start us, length us, event | category | flops | bytes accessed | tf_op | source)
XLA Modules:
  0.0 210.1 jit_solution(7868595405274421942)
XLA Ops:
  0.0 0.5 collective-permute-start.2
  0.5 0.0 collective-permute-start.3
  0.5 3.0 %collective-permute-start = (bf16[256,1280]{1,0:T(8,128)(2,1)}, bf16[256,1280]{1,0:T(8,128)(2,1)}, u32[]{:S(2)}, u32[]{:S(2)}) collective-permute-start(bf16[256,1280]{1,0:T(8,128)(2,1)} %refs_1_.3), channel_id=1, source_target_pairs={{0,8},{4,12},{8,0},{12,4},{1,9},{5,13},{9,1},{13,5},{2,10},{6,14},... | collective-permute-start | bytes 1966088 | tf_op jit(solution)/shard_map/ppermute | solution.py:156
  3.5 0.0 collective-permute-start.1
  4.1 1.3 reshape.16.gain
  5.4 13.3 %attend.3 = (f32[256,1280]{1,0:T(8,128)}, f32[2,2,5,256]{3,2,1,0:T(8,128)}) custom-call(s32[1]{0:T(128)S(6)} %copy.14.refs_0_, bf16[256,1280]{1,0:T(8,128)(2,1)} %refs_1_.3, bf16[2048,256]{1,0:T(8,128)(2,1)} %refs_3_.3, bf16[2048,256]{1,0:T(8,128)(2,1)} %refs_4_.1), custom_call_target="tpu_custom_call" | custom-call | flops 2684354560 | bytes 4063232 | tf_op jit(solution)/shard_map/attend/pallas_call | solution.py:118
  18.7 0.0 collective-permute-done.refs_2_
  18.7 0.0 collective-permute-done.1.refs_1_.refs_0_
  18.7 0.0 collective-permute-done.2.refs_5_.refs_2_
  18.7 0.0 collective-permute-done.3.refs_6_.refs_3_
  18.7 21.6 %attend.4 = (bf16[256,1280]{1,0:T(8,128)(2,1)}, f32[2,2,5,256]{3,2,1,0:T(8,128)}) custom-call(s32[1]{0:T(128)S(6)} %copy.14.refs_0_, s32[1]{0:T(128)} %collective-permute-done.1.refs_1_.refs_0_, bf16[256,1280]{1,0:T(8,128)(2,1)} %collective-permute-done.refs_2_, bf16[2048,256]{1,0:T(8,128)(2,1)} %refs_3_.3, bf16[2048,256]{1,0:T(8,128)(2,1)} %refs_4_.1, ...), custom_call_target="tpu_custom_call" | custom-call | flops 5368709120 | bytes 6160384 | tf_op jit(solution)/shard_map/attend/pallas_call | solution.py:118
  40.3 0.1 collective-permute-start.5
  40.4 1.2 broadcast_compare_fusion
  41.6 1.3 multiply_add_fusion
  42.9 2.0 collective-permute-start.4
  44.9 12.9 %attend.5 = (f32[256,1280]{1,0:T(8,128)}, f32[2,2,5,256]{3,2,1,0:T(8,128)}) custom-call(s32[1]{0:T(128)} %collective-permute-done.1.refs_1_.refs_0_, bf16[256,1280]{1,0:T(8,128)(2,1)} %refs_1_.3, bf16[2048,256]{1,0:T(8,128)(2,1)} %collective-permute-done.2.refs_5_.refs_2_, bf16[2048,256]{1,0:T(8,128)(2,1)} %collective-permute-done.3.refs_6_.refs_3_), custom_call_target="tpu_custom_call" | custom-call | flops 2684354560 | bytes 4063232 | tf_op jit(solution)/shard_map/attend/pallas_call | solution.py:118
  57.8 0.0 collective-permute-done.4.refs_1_
  57.8 0.0 collective-permute-done.5.refs_4_
  57.8 3.4 %merge.1.own = bf16[256,1280]{1,0:T(8,128)(2,1)} custom-call(f32[2,2,5,256]{3,2,1,0:T(8,128)} %get-tuple-element.19.refs_0_, f32[2,2,5,256]{3,2,1,0:T(8,128)} %collective-permute-done.4.refs_1_, f32[2,2,5,256]{3,2,1,0:T(8,128)} %get-tuple-element.22.refs_2_, f32[256,1280]{1,0:T(8,128)} %get-tuple-element.23.refs_3_, ...), custom_call_target="tpu_custom_call" | custom-call | tf_op jit(solution)/shard_map/merge/pallas_call | solution.py:198
  61.2 64.1 %project.1 = (f32[256,1280]{1,0:T(8,128)}, bf16[4,128,1280]{2,1,0:T(8,128)(2,1)}, f32[1,256]{1,0:T(1,128)}) custom-call(bf16[256,1280]{1,0:T(8,128)(2,1)} %merge.1.own, bf16[1280,1280]{1,0:T(8,128)(2,1)} %weight_hbm.1, bf16[256,1280]{1,0:T(8,128)(2,1)} %residual_hbm.1, f32[1,1280]{1,0:T(1,128)} %reshape.16.gain, f32[4,1280]{1,0:T(4,128)} %bitcast.7, ...), custom_call_target="tpu_custom_call" | custom-call | tf_op jit(solution)/shard_map/project/pallas_call | solution.py:937
  125.3 81.7 %experts.1 = bf16[4,128,1280]{2,1,0:T(8,128)(2,1)} custom-call(bf16[4,128,1280]{2,1,0:T(8,128)(2,1)} %get-tuple-element.28.packed, bf16[1,5120,1024]{2,1,0:T(8,128)(2,1)} %gate_hbm.1, bf16[1,5120,1024]{2,1,0:T(8,128)(2,1)} %up_hbm.1, bf16[1,1024,5120]{2,1,0:T(8,128)(2,1)} %down_hbm.1), custom_call_target="tpu_custom_call" | custom-call | tf_op jit(solution)/shard_map/experts/pallas_call | solution.py:653
  207.1 0.0 copy-start
  207.1 0.0 copy-start.1
  207.1 2.0 fusion.1
  209.1 0.0 copy-done
  209.1 0.0 copy-done.1
  209.1 1.0 add_convert_fusion
Async XLA Ops:
  0.0 18.7 %collective-permute-start.2 = (bf16[2048,256]{1,0:T(8,128)(2,1)}, bf16[2048,256]{1,0:T(8,128)(2,1)}, u32[]{:S(2)}, u32[]{:S(2)}) collective-permute-start(bf16[2048,256]{1,0:T(8,128)(2,1)} %refs_3_.3), channel_id=1, source_target_pairs={{0,4},{4,0},{8,12},{12,8},{1,5},{5,1},{9,13},{13,9},{2,6},{6,2},{1... | collective-permute-start | bytes 3145736 | tf_op jit(solution)/shard_map/ppermute | solution.py:157
  0.5 18.2 %collective-permute-start.3 = (bf16[2048,256]{1,0:T(8,128)(2,1)}, bf16[2048,256]{1,0:T(8,128)(2,1)}, u32[]{:S(2)}, u32[]{:S(2)}) collective-permute-start(bf16[2048,256]{1,0:T(8,128)(2,1)} %refs_4_.1), channel_id=1, source_target_pairs={{0,4},{4,0},{8,12},{12,8},{1,5},{5,1},{9,13},{13,9},{2,6},{6,2},{1... | collective-permute-start | bytes 3145736 | tf_op jit(solution)/shard_map/ppermute | solution.py:158
  0.5 18.2 %collective-permute-start = (bf16[256,1280]{1,0:T(8,128)(2,1)}, bf16[256,1280]{1,0:T(8,128)(2,1)}, u32[]{:S(2)}, u32[]{:S(2)}) collective-permute-start(bf16[256,1280]{1,0:T(8,128)(2,1)} %refs_1_.3), channel_id=1, source_target_pairs={{0,8},{4,12},{8,0},{12,4},{1,9},{5,13},{9,1},{13,5},{2,10},{6,14},... | collective-permute-start | bytes 1966088 | tf_op jit(solution)/shard_map/ppermute | solution.py:156
  3.5 15.2 %collective-permute-start.1 = (s32[1]{0:T(128)}, s32[1]{0:T(128)}, u32[]{:S(2)}, u32[]{:S(2)}) collective-permute-start(s32[1]{0:T(128)} %param.16), channel_id=1, source_target_pairs={{0,4},{4,0},{8,12},{12,8},{1,5},{5,1},{9,13},{13,9},{2,6},{6,2},{1... | collective-permute-start | bytes 20 | tf_op jit(solution)/shard_map/ppermute | solution.py:159
  40.3 17.5 %collective-permute-start.5 = (bf16[256,1280]{1,0:T(8,128)(2,1)}, bf16[256,1280]{1,0:T(8,128)(2,1)}, u32[]{:S(2)}, u32[]{:S(2)}) collective-permute-start(bf16[256,1280]{1,0:T(8,128)(2,1)} %get-tuple-element.24), channel_id=1, source_target_pairs={{8,0},{12,4},{0,8},{4,12},{9,1},{13,5},{1,9},{5,13},{10,2},{14,6},... | collective-permute-start | bytes 1966088 | tf_op jit(solution)/shard_map/ppermute | solution.py:170
  42.9 14.9 %collective-permute-start.4 = (f32[2,2,5,256]{3,2,1,0:T(8,128)}, f32[2,2,5,256]{3,2,1,0:T(8,128)}, u32[]{:S(2)}, u32[]{:S(2)}) collective-permute-start(f32[2,2,5,256]{3,2,1,0:T(8,128)} %get-tuple-element.21), channel_id=1, source_target_pairs={{8,0},{12,4},{0,8},{4,12},{9,1},{13,5},{1,9},{5,13},{10,2},{14,6},... | collective-permute-start | bytes 61448 | tf_op jit(solution)/shard_map/ppermute | solution.py:170
  207.1 2.0 copy-start
  207.1 2.0 copy-start.1
